TPU v7x, 128 devices: a whole 4x4x4 slice. The times are simulated.
128 devices in a mesh: dp: 16 (over z, y_hi, core), tensor: 8 (over x, y_lo).
Axes of the slice: x: 4, y: 4 (y_hi: 2, y_lo: 2; y = y_hi * 2 + y_lo), z: 4, core: 2. Of those that a mesh axis runs over, the one named last changes fastest.
Arguments:
- history: bfloat16 [4, 3072, 4096], P(None, 'dp'), may hold values from -6 to 6
- depth_weights: float32 [4], replicated, may hold values from 0.2 to 1
- depth_index: int32 [4], replicated, may hold values from 0 to 3
- gain: float32 [4096], replicated, may hold values from 0.1 to 1.9
- gate_blocks: bfloat16 [896, 128, 128], P(('tensor', 'dp')), may hold values from -0.1875 to 0.1875
- up_blocks: bfloat16 [896, 128, 128], P(('tensor', 'dp')), may hold values from -0.1875 to 0.1875
- down_blocks: bfloat16 [896, 128, 128], P(('tensor', 'dp')), may hold values from -0.09375 to 0.09375
- block_ids: int32 [896, 2], P('tensor'), may hold values from 0 to 31, as said below
- grad_out: bfloat16 [3072, 4096], P('dp'), may hold values from -16 to 16
Outputs:
- layer_out: bfloat16 [3072, 4096], P('dp', 'tensor')
- grad_mixed: float32 [3072, 4096], P('dp', 'tensor')
- grad_gate: float32 [896, 128, 128], P(('tensor', 'dp'))
- grad_up: float32 [896, 128, 128], P(('tensor', 'dp'))
- grad_down: float32 [896, 128, 128], P(('tensor', 'dp'))
- grad_depth: float32 [4], replicated
- grad_gain: float32 [4096], P('tensor')
Inputs may be any that keep to these rules, and one draw needn't show every extreme that they name: `block_ids`: within the 112 rows of one index of tensor the pairs are distinct; column 0 is a row block below 32, column 1 a column block below 14 counted within that index's hidden units.
All inputs are finite; a program needn't handle non-finite values.
Results may differ from a plain program's by a relative error of at most 0.025.
Values may be sent and summed in bfloat16 or wider, within the bound.
No kernel may reach another device: no remote copies, remote signals or barrier semaphores. Data moves between devices by JAX's collectives and lax.ppermute only.
A program may use at most 192 MiB of HBM per device.

v0:
```python
import jax
import jax.numpy as jnp
from jax import lax
from jax.sharding import PartitionSpec as P

FF = 14336
EPSILON = 1e-05


def norm_rows(mixed, gain):
    scale_inv = lax.rsqrt(jnp.mean(mixed * mixed, axis=-1, keepdims=True) + EPSILON)
    return mixed * scale_inv * gain


def per_device(
    history,
    depth_weights,
    depth_index,
    gain,
    gate_blocks,
    up_blocks,
    down_blocks,
    block_ids,
    grad_out,
):
    tok_rows = history.shape[1]
    width = history.shape[2]
    block_size = gate_blocks.shape[1]
    row_blocks = width // block_size
    tensor_count = lax.axis_size("tensor")
    col_blocks = FF // block_size // tensor_count
    share_width = width // tensor_count
    share_start = lax.axis_index("tensor") * share_width
    mixed = jnp.zeros((tok_rows, width), jnp.float32)
    for layer_slot in range(depth_index.shape[0]):
        earlier = lax.dynamic_index_in_dim(history, depth_index[layer_slot], 0, keepdims=False)
        mixed = mixed + depth_weights[layer_slot] * earlier.astype(jnp.float32)
    scale_inv = lax.rsqrt(jnp.mean(mixed * mixed, axis=-1, keepdims=True) + EPSILON)
    normed = (mixed * scale_inv * gain).astype(jnp.bfloat16)
    normed3 = normed.reshape(tok_rows, row_blocks, block_size)
    out3 = grad_out.reshape(tok_rows, row_blocks, block_size)
    row_ids = block_ids[:, 0]
    col_ids = block_ids[:, 1]
    zero_cols = jnp.zeros((tok_rows, col_blocks, block_size), jnp.float32)
    zero_rows = jnp.zeros((tok_rows, row_blocks, block_size), jnp.float32)

    def select():
        return (row_ids, col_ids)

    gate_all, up_all, down_all = (
        lax.all_gather(gate_blocks, "dp", axis=0, tiled=True),
        lax.all_gather(up_blocks, "dp", axis=0, tiled=True),
        lax.all_gather(down_blocks, "dp", axis=0, tiled=True),
    )
    pieces = (gate_all, up_all)
    rows_here, cols_here = select()
    picked = jnp.take(normed3, rows_here, axis=1)
    gate_part = jnp.einsum("tbi,bij->tbj", picked, pieces[0], preferred_element_type=jnp.float32)
    up_part = jnp.einsum("tbi,bij->tbj", picked, pieces[1], preferred_element_type=jnp.float32)
    gate_pre = zero_cols.at[:, cols_here].add(gate_part)
    up_pre = zero_cols.at[:, cols_here].add(up_part)
    hidden = (jax.nn.silu(gate_pre) * up_pre).astype(jnp.bfloat16)
    rows_here, cols_here = select()
    picked = jnp.take(hidden, cols_here, axis=1)
    product = jnp.einsum("tbi,bij->tbj", picked, down_all, preferred_element_type=jnp.float32)
    ffn3 = zero_rows.at[:, rows_here].add(product)
    ffn_share = lax.psum_scatter(
        ffn3.reshape(tok_rows, width).astype(jnp.bfloat16),
        "tensor",
        scatter_dimension=1,
        tiled=True,
    ).astype(jnp.float32)
    mixed_share = lax.dynamic_slice_in_dim(mixed, share_start, share_width, 1)
    layer_out = (mixed_share + ffn_share).astype(jnp.bfloat16)
    rows_here, cols_here = select()
    picked = jnp.take(out3, rows_here, axis=1)
    product = jnp.einsum("tbj,bij->tbi", picked, down_all, preferred_element_type=jnp.float32)
    grad_hidden = zero_cols.at[:, cols_here].add(product)
    sigmoid_gate = jax.nn.sigmoid(gate_pre)
    grad_gate_pre = (
        grad_hidden * up_pre * sigmoid_gate * (1.0 + gate_pre * (1.0 - sigmoid_gate))
    ).astype(jnp.bfloat16)
    grad_up_pre = (grad_hidden * gate_pre * sigmoid_gate).astype(jnp.bfloat16)
    pieces = (gate_all, up_all)
    rows_here, cols_here = select()
    picked_gate = jnp.take(grad_gate_pre, cols_here, axis=1)
    picked_up = jnp.take(grad_up_pre, cols_here, axis=1)
    contrib = jnp.einsum("tbj,bij->tbi", picked_gate, pieces[0], preferred_element_type=jnp.float32)
    contrib = contrib + jnp.einsum(
        "tbj,bij->tbi", picked_up, pieces[1], preferred_element_type=jnp.float32
    )
    grad_normed3 = zero_rows.at[:, rows_here].add(contrib)
    rows_here, cols_here = select()
    picked_in = jnp.take(normed3, rows_here, axis=1)
    picked_out = jnp.take(out3, rows_here, axis=1)
    picked_gate = jnp.take(grad_gate_pre, cols_here, axis=1)
    picked_up = jnp.take(grad_up_pre, cols_here, axis=1)
    picked_hidden = jnp.take(hidden, cols_here, axis=1)
    gate_term = jnp.einsum(
        "tbi,tbj->bij", picked_in, picked_gate, preferred_element_type=jnp.float32
    )
    up_term = jnp.einsum("tbi,tbj->bij", picked_in, picked_up, preferred_element_type=jnp.float32)
    down_term = jnp.einsum(
        "tbi,tbj->bij", picked_hidden, picked_out, preferred_element_type=jnp.float32
    )
    block_grads = lax.psum_scatter(
        jnp.stack([gate_term, up_term, down_term], axis=1).astype(jnp.bfloat16),
        "dp",
        scatter_dimension=0,
        tiled=True,
    ).astype(jnp.float32)
    grad_normed = grad_normed3.reshape(tok_rows, width)
    full_grad = lax.psum(grad_normed.astype(jnp.bfloat16), "tensor").astype(jnp.float32)
    ignored, pull_back = jax.vjp(norm_rows, mixed, gain)
    grad_x, gain_rows = pull_back(full_grad)
    grad_full = grad_out.astype(jnp.float32) + grad_x
    grad_mixed = lax.dynamic_slice_in_dim(grad_full, share_start, share_width, 1)
    gain_part = lax.dynamic_slice_in_dim(gain_rows, share_start, share_width, 0)
    depth_list = []
    for layer_slot in range(depth_index.shape[0]):
        earlier = lax.dynamic_index_in_dim(history, depth_index[layer_slot], 0, keepdims=False)
        depth_list.append(jnp.sum(grad_full * earlier.astype(jnp.float32)))
    gain_sum, depth_sum = lax.psum((gain_part, jnp.stack(depth_list)), "dp")
    return (
        layer_out,
        grad_mixed,
        block_grads[:, 0],
        block_grads[:, 1],
        block_grads[:, 2],
        depth_sum,
        gain_sum,
    )


def solution(mesh):
    placed = (
        P(None, "dp", None),
        P(),
        P(),
        P(),
        P(("tensor", "dp"), None, None),
        P(("tensor", "dp"), None, None),
        P(("tensor", "dp"), None, None),
        P("tensor", None),
        P("dp", None),
    )
    return jax.shard_map(
        per_device,
        mesh=mesh,
        in_specs=placed,
        out_specs=(
            P("dp", "tensor"),
            P("dp", "tensor"),
            P(("tensor", "dp"), None, None),
            P(("tensor", "dp"), None, None),
            P(("tensor", "dp"), None, None),
            P(),
            P("tensor"),
        ),
        check_vma=False,
    )
```

profile of v0, /device:TPU:0, one launch (start us, length us, event | category | flops | bytes accessed | tf_op | source)
XLA Modules:
  0.0 650.3 jit_solution(3859835161289719291)
XLA Ops:
  7.2 0.0 all-gather.4.cloned.1.call-start
  7.2 0.7 all-gather.4.cloned.1.call-update
  7.9 0.0 all-gather.6.cloned.1.call-start
  7.9 0.7 all-gather.6.cloned.1.call-update
  8.7 0.0 all-gather.8.cloned.1.call-start
  8.7 0.7 all-gather.8.cloned.1.call-update
  9.4 0.0 all-reduce.5.cloned.1.call-start
  9.4 1.4 fusion.74
  18.6 1.4 fusion.75
  20.0 7.3 %fusion.43 = f32[24,8,32,128]{3,1,2,0:T(8,128)S(1)} fusion(f32[]{:T(128)} %bitcast.9, f32[]{:T(128)} %bitcast.6, f32[]{:T(128)} %bitcast.3, f32[]{:T(128)} %bitcast, bf16[4,192,4096]{2,1,0:T(8,128)(2,1)} %param.13, s32[]{:T(128)S(6)} %select_n.49, s32[]{:T(128)S(6)} %select_n.48, s32[]{:T(128)S(6)} %select_n.47, s32[]{:T(128)S(6)} %select_n.46), kind=kLoop, calls=%fused_computation.71 | loop fusion | flops 8650752 | bytes 9437216
  27.3 0.5 copy.31
  27.9 0.1 copy-done.8
  28.1 5.6 multiply_reduce_fusion
  33.6 2.0 fusion.49
  35.7 3.8 gather_fusion
  39.5 0.4 copy_bitcast_fusion.2
  39.9 3.7 gather_fusion.2
  43.7 22.0 %all-gather.4.cloned.1.call-done = bf16[112,128,128]{2,1,0:T(8,128)(2,1)} async-done(((bf16[7,128,128]{2,1,0:T(8,128)(2,1)}), bf16[112,128,128]{2,1,0:T(8,128)(2,1)}) %all-gather.4.cloned.1.call-update) | async-done | bytes 3670032 | tf_op jit(solution)/shard_map/all_gather | solution.py:51
  65.7 9.4 %fusion.19 = f32[112,192,128]{2,1,0:T(8,128)} fusion(bf16[112,128,128]{2,1,0:T(8,128)(2,1)} %all-gather.4.cloned.1.call-done, bf16[112,192,128]{2,1,0:T(8,128)(2,1)} %gather_fusion, pred[112]{0:T(512)(128)(4,1)S(1)} %get-tuple-element.30), kind=kOutput, calls=%fused_computation.30 | convolution fusion | flops 707395584 | bytes 20185200 | tf_op jit(solution)/shard_map/tbi,bij->tbj/dot_general | solution.py:58
  75.1 0.1 broadcast_in_dim.37.clone
  75.2 18.7 %scatter_fusion = f32[192,14,128]{2,0,1:T(8,128)S(1)} fusion(f32[192,14,128]{2,0,1:T(8,128)S(1)} %broadcast_in_dim.37.clone, s32[112]{0:T(128)S(1)} %get-tuple-element.32, f32[112,192,128]{2,1,0:T(8,128)} %fusion.19), kind=kCustom, calls=%fused_computation.5 | custom fusion | flops 2752512 | bytes 33030592 | tf_op jit(solution)/shard_map/scatter-add | solution.py:60
  93.9 25.2 %all-gather.6.cloned.1.call-done = bf16[112,128,128]{2,1,0:T(8,128)(2,1)} async-done(((bf16[7,128,128]{2,1,0:T(8,128)(2,1)}), bf16[112,128,128]{2,1,0:T(8,128)(2,1)}) %all-gather.6.cloned.1.call-update) | async-done | bytes 3670032 | tf_op jit(solution)/shard_map/all_gather | solution.py:52
  119.1 9.4 %fusion.17 = f32[112,192,128]{2,1,0:T(8,128)} fusion(bf16[112,128,128]{2,1,0:T(8,128)(2,1)} %all-gather.6.cloned.1.call-done, bf16[112,192,128]{2,1,0:T(8,128)(2,1)} %gather_fusion, pred[112]{0:T(512)(128)(4,1)S(1)} %get-tuple-element.30), kind=kOutput, calls=%fused_computation.28 | convolution fusion | flops 707395584 | bytes 20185200 | tf_op jit(solution)/shard_map/tbi,bij->tbj/dot_general | solution.py:59
  128.6 0.1 broadcast_in_dim.37.clone.2
  128.7 18.3 %scatter_fusion.1 = f32[192,14,128]{2,0,1:T(8,128)S(1)} fusion(f32[192,14,128]{2,0,1:T(8,128)S(1)} %broadcast_in_dim.37.clone.2, s32[112]{0:T(128)S(1)} %get-tuple-element.32, f32[112,192,128]{2,1,0:T(8,128)} %fusion.17), kind=kCustom, calls=%fused_computation.6 | custom fusion | flops 2752512 | bytes 33030592 | tf_op jit(solution)/shard_map/scatter-add | solution.py:61
  147.0 25.6 %all-gather.8.cloned.1.call-done = bf16[112,128,128]{2,1,0:T(8,128)(2,1)} async-done(((bf16[7,128,128]{2,1,0:T(8,128)(2,1)}), bf16[112,128,128]{2,1,0:T(8,128)(2,1)}) %all-gather.8.cloned.1.call-update) | async-done | bytes 3670032 | tf_op jit(solution)/shard_map/all_gather | solution.py:53
  172.6 10.2 %fusion.10 = f32[112,192,128]{2,1,0:T(8,128)} fusion(bf16[112,128,128]{2,1,0:T(8,128)(2,1)} %all-gather.8.cloned.1.call-done, bf16[112,192,128]{2,1,0:T(8,128)(2,1)} %gather_fusion.2, pred[112]{0:T(512)(128)(4,1)S(1)} %get-tuple-element.30), kind=kOutput, calls=%fused_computation.21 | convolution fusion | flops 707395584 | bytes 20185200 | tf_op jit(solution)/shard_map/tbj,bij->tbi/dot_general | solution.py:77
  182.9 0.1 broadcast_in_dim.37.clone.1
  183.0 18.4 %scatter_fusion.3 = f32[192,14,128]{2,0,1:T(8,128)S(1)} fusion(f32[192,14,128]{2,0,1:T(8,128)S(1)} %broadcast_in_dim.37.clone.1, s32[112]{0:T(128)S(1)} %get-tuple-element.32, f32[112,192,128]{2,1,0:T(8,128)} %fusion.10), kind=kCustom, calls=%fused_computation.8 | custom fusion | flops 2752512 | bytes 33030592 | tf_op jit(solution)/shard_map/scatter-add | solution.py:78
  201.4 3.3 multiply_convert_fusion.1
  204.7 4.9 gather_fusion.4
  209.5 3.8 gather_fusion.3
  213.3 10.4 %fusion.2 = f32[112,192,128]{2,1,0:T(8,128)} fusion(bf16[112,128,128]{2,1,0:T(8,128)(2,1)} %all-gather.6.cloned.1.call-done, bf16[112,192,128]{2,1,0:T(8,128)(2,1)} %gather_fusion.4, pred[112]{0:T(512)(128)(4,1)S(1)} %get-tuple-element.18), kind=kOutput, calls=%fused_computation.13 | convolution fusion | flops 707395584 | bytes 20185200 | tf_op jit(solution)/shard_map/tbj,bij->tbi/dot_general | solution.py:89
  223.7 12.0 %fusion.29 = f32[112,192,128]{2,1,0:T(8,128)} fusion(f32[112,192,128]{2,1,0:T(8,128)} %fusion.2, bf16[112,128,128]{2,1,0:T(8,128)(2,1)} %all-gather.4.cloned.1.call-done, bf16[112,192,128]{2,1,0:T(8,128)(2,1)S(1)} %copy-done.3, pred[112]{0:T(512)(128)(4,1)S(1)} %get-tuple-element.18), kind=kOutput, calls=%fused_computation.56 | convolution fusion | flops 710148096 | bytes 31195248 | tf_op jit(solution)/shard_map/tbj,bij->tbi/dot_general | solution.py:88
  235.7 0.3 broadcast_in_dim.36.clone.1
  236.0 18.3 %scatter_fusion.4 = f32[192,32,128]{2,0,1:T(8,128)S(1)} fusion(f32[192,32,128]{2,0,1:T(8,128)S(1)} %broadcast_in_dim.36.clone.1, s32[112]{0:T(128)S(1)} %get-tuple-element.33, f32[112,192,128]{2,1,0:T(8,128)} %fusion.29), kind=kCustom, calls=%fused_computation.9 | custom fusion | flops 2752512 | bytes 33030592 | tf_op jit(solution)/shard_map/scatter-add | solution.py:92
  254.3 1.4 copy_bitcast_fusion
  255.7 0.0 all-reduce.5.cloned.1.call-update
  255.7 0.0 reduce-scatter.5.cloned.1.call-start
  255.8 1.0 copy-done.1
  256.8 3.8 gather_fusion.1
  260.6 9.6 %fusion.13 = f32[112,192,128]{2,1,0:T(8,128)} fusion(bf16[112,128,128]{2,1,0:T(8,128)(2,1)} %all-gather.8.cloned.1.call-done, bf16[112,192,128]{2,1,0:T(8,128)(2,1)} %gather_fusion.1, pred[112]{0:T(512)(128)(4,1)S(1)} %get-tuple-element.18), kind=kOutput, calls=%fused_computation.24 | convolution fusion | flops 707395584 | bytes 20185200 | tf_op jit(solution)/shard_map/tbi,bij->tbj/dot_general | solution.py:65
  270.2 0.3 broadcast_in_dim.36.clone
  270.6 18.5 %scatter_fusion.2 = f32[192,32,128]{2,0,1:T(8,128)S(1)} fusion(f32[192,32,128]{2,0,1:T(8,128)S(1)} %broadcast_in_dim.36.clone, s32[112]{0:T(128)S(1)} %get-tuple-element.33, f32[112,192,128]{2,1,0:T(8,128)} %fusion.13), kind=kCustom, calls=%fused_computation.7 | custom fusion | flops 2752512 | bytes 33030592 | tf_op jit(solution)/shard_map/scatter-add | solution.py:66
  289.1 1.4 copy_bitcast_fusion.1
  290.5 0.0 reduce-scatter.5.cloned.1.call-update
  290.5 0.0 all-reduce.7.cloned.1.call-start
  290.6 8.7 %convert_bitcast_fusion.5 = bf16[112,1,128,128]{3,2,0,1:T(8,128)(2,1)} fusion(bf16[112,192,128]{2,1,0:T(8,128)(2,1)} %gather_fusion.4, pred[112]{0:T(512)(128)(4,1)S(1)} %get-tuple-element.18, bf16[112,192,128]{2,1,0:T(8,128)(2,1)} %gather_fusion, pred[112]{0:T(512)(128)(4,1)S(1)} %get-tuple-element.30), kind=kOutput, calls=%fused_computation.60 | convolution fusion | flops 711983104 | bytes 14680288 | tf_op jit(solution)/shard_map/tbi,tbj->bij/dot_general | solution.py:102
  299.3 8.8 %convert_bitcast_fusion.6 = bf16[112,1,128,128]{3,2,0,1:T(8,128)(2,1)} fusion(bf16[112,192,128]{2,1,0:T(8,128)(2,1)} %gather_fusion.3, pred[112]{0:T(512)(128)(4,1)S(1)} %get-tuple-element.18, bf16[112,192,128]{2,1,0:T(8,128)(2,1)} %gather_fusion, pred[112]{0:T(512)(128)(4,1)S(1)} %get-tuple-element.30), kind=kOutput, calls=%fused_computation.61 | convolution fusion | flops 711983104 | bytes 14680288 | tf_op jit(solution)/shard_map/tbi,tbj->bij/dot_general | solution.py:99
  308.2 4.5 convert_bitcast_fusion.4
  312.7 9.7 %pad_maximum_fusion = bf16[112,3,128,128]{3,2,0,1:T(8,128)(2,1)} fusion(bf16[112,1,128,128]{3,2,0,1:T(8,128)(2,1)} %convert_bitcast_fusion.4, bf16[112,1,128,128]{3,2,0,1:T(8,128)(2,1)} %convert_bitcast_fusion.5, bf16[112,1,128,128]{3,2,0,1:T(8,128)(2,1)} %convert_bitcast_fusion.6), kind=kLoop, calls=%fused_computation.10 | loop fusion | flops 11010048 | bytes 22020096 | tf_op jit(solution)/shard_map/stack | solution.py:107
  322.5 0.6 copy-done.9
  323.1 0.6 dynamic-slice.2
  323.7 18.1 %all-reduce.5.cloned.1.call-done = bf16[192,4096]{1,0:T(8,128)(2,1)} async-done(((bf16[192,4096]{1,0:T(8,128)(2,1)}), bf16[192,4096]{1,0:T(8,128)(2,1)}) %all-reduce.5.cloned.1.call-update) | async-done | bytes 1572880 | tf_op jit(solution)/shard_map/psum | solution.py:113
  341.8 2.8 fusion.35
  344.6 0.1 dynamic_slice.32
  344.7 5.9 fusion.39
  350.6 2.7 pad_maximum_fusion.1
  353.9 37.3 %all-reduce.1 = (f32[4]{0:T(128)}, f32[512]{0:T(512)}) all-reduce(f32[4]{0:T(128)S(1)} %pad_maximum_fusion.1, f32[512]{0:T(512)S(1)} %dynamic_slice.32), channel_id=1, replica_groups=mesh['dp'=16,'tensor'=8] {'dp'}, use_global_device_ids=true, to_apply=%region_14.17 | all-reduce | flops 516 | bytes 4128 | tf_op jit(solution)/shard_map/psum | solution.py:123
  391.2 1.8 constant_dynamic-slice_fusion
  393.0 1.6 add_convert_fusion
  394.7 246.3 %all-reduce.7.cloned.1.call-done = bf16[112,3,128,128]{3,2,0,1:T(8,128)(2,1)} async-done(((bf16[112,3,128,128]{3,2,0,1:T(8,128)(2,1)}), bf16[112,3,128,128]{3,2,0,1:T(8,128)(2,1)}) %all-reduce.7.cloned.1.call-update) | async-done | bytes 11010064
  640.9 1.2 dynamic-slice_convert_fusion
  642.2 1.1 slice_bitcast_fusion
  (39 shorter events, 0.1 us)
Async XLA Ops:
  7.2 58.5 %all-gather.4.cloned.1.call-start = ((), (), s32[]{:S(2)}) async-start(), calls=%async_computation.1 | async-start | bytes 3899392 | tf_op jit(solution)/shard_map/all_gather | solution.py:51
  7.9 111.2 %all-gather.6.cloned.1.call-start = ((), (), s32[]{:S(2)}) async-start(), calls=%async_computation.2 | async-start | bytes 3899392 | tf_op jit(solution)/shard_map/all_gather | solution.py:52
  8.7 164.0 %all-gather.8.cloned.1.call-start = ((), (), s32[]{:S(2)}) async-start(), calls=%async_computation.3 | async-start | bytes 3899392 | tf_op jit(solution)/shard_map/all_gather | solution.py:53
  9.4 332.4 %all-reduce.5.cloned.1.call-start = ((), (), s32[]{:S(2)}) async-start(), calls=%async_computation.5 | async-start | bytes 3145728 | tf_op jit(solution)/shard_map/psum | solution.py:113
  20.0 8.0 %slice-start = ((s8[6291456]{0:T(1024)(128)(4,1)}), s8[4194304]{0:T(1024)(128)(4,1)S(1)}, s32[]{:S(2)}) async-start(s8[6291456]{0:T(1024)(128)(4,1)} %bitcast.158), calls=%async_computation.7 | async-start | bytes 8388608
  20.0 8.0 %slice-start.1 = ((s8[6291456]{0:T(1024)(128)(4,1)}), s8[2097152]{0:T(1024)(128)(4,1)S(1)}, s32[]{:S(2)}) async-start(s8[6291456]{0:T(1024)(128)(4,1)} %bitcast.158), calls=%async_computation.8 | async-start | bytes 4194304
  27.3 0.7 copy-start.8
  28.0 5.6 copy-start.7
  35.7 3.8 copy-start.4
  147.0 25.6 %copy-start = (f32[192,14,128]{2,0,1:T(8,128)}, f32[192,14,128]{2,0,1:T(8,128)S(1)}, u32[]{:S(2)}) copy-start(f32[192,14,128]{2,0,1:T(8,128)S(1)} %scatter_fusion.1) | copy-start | bytes 4128772
  213.3 10.4 %copy-start.3 = (bf16[112,192,128]{2,1,0:T(8,128)(2,1)S(1)}, bf16[112,192,128]{2,1,0:T(8,128)(2,1)}, u32[]{:S(2)}) copy-start(bf16[112,192,128]{2,1,0:T(8,128)(2,1)} %gather_fusion.3) | copy-start | bytes 16515076
  255.7 1.1 copy-start.1
  255.7 137.3 %reduce-scatter.5.cloned.1.call-start = ((), (), s32[]{:S(2)}) async-start(), calls=%async_computation.4 | async-start | bytes 1769472 | tf_op jit(solution)/shard_map/reduce_scatter | solution.py:67
  290.5 350.4 %all-reduce.7.cloned.1.call-start = ((), (), s32[]{:S(2)}) async-start(), calls=%async_computation.6 | async-start | bytes 22020096
  290.6 17.6 %slice-start.2 = ((s8[5505024]{0:T(1024)(128)(4,1)}), s8[4194304]{0:T(1024)(128)(4,1)S(1)}, s32[]{:S(2)}) async-start(s8[5505024]{0:T(1024)(128)(4,1)} %bitcast.160), calls=%async_computation.9 | async-start | bytes 8388608
  290.6 17.6 %slice-start.4 = ((s8[5505024]{0:T(1024)(128)(4,1)}), s8[4194304]{0:T(1024)(128)(4,1)S(1)}, s32[]{:S(2)}) async-start(s8[5505024]{0:T(1024)(128)(4,1)} %bitcast.162), calls=%async_computation.11 | async-start | bytes 8388608
  299.3 8.8 %slice-start.3 = ((s8[5505024]{0:T(1024)(128)(4,1)}), s8[1310720]{0:T(1024)(128)(4,1)S(1)}, s32[]{:S(2)}) async-start(s8[5505024]{0:T(1024)(128)(4,1)} %bitcast.160), calls=%async_computation.10 | async-start | bytes 2621440
  299.3 8.8 %slice-start.5 = ((s8[5505024]{0:T(1024)(128)(4,1)}), s8[1310720]{0:T(1024)(128)(4,1)S(1)}, s32[]{:S(2)}) async-start(s8[5505024]{0:T(1024)(128)(4,1)} %bitcast.162), calls=%async_computation.12 | async-start | bytes 2621440
  322.4 0.7 copy-start.9
  322.4 19.4 %copy-start.2 = (f32[192,4096]{1,0:T(8,128)S(1)}, f32[192,4096]{1,0:T(8,128)}, u32[]{:S(2)}) copy-start(f32[192,4096]{1,0:T(8,128)} %get-tuple-element.23) | copy-start | bytes 9437188
  341.8 2.9 copy-start.5
  341.8 2.9 copy-start.6
Sparse Core Ops, SparseCore 0:
  10.4 55.1 all-gather.3
  68.1 50.9 all-gather.5
  121.6 50.9 all-gather.7
  255.8 85.9 all-reduce.4
  344.1 44.9 reduce-scatter.4
  391.5 249.4 all-reduce.6
where the time goes:
time: 659 us; the launch traced here: 650 us
  waiting for transfers between devices  339 us (51%)
  other arithmetic  137 us (21%)
  matrix products  83.2 us (13%)
  blocking collectives  37.3 us (6%)
  local copies, waits for them, and re-layouts  30.1 us (5%)
  between operations  23 us (3%)
    unnamed x7, waiting for transfers between devices  248 us
    psum x1, blocking collectives, per_device(): gain_sum, depth_sum = lax.psum((gain_part, jnp.stack(depth_list)), 'dp')  37.3 us
    all_gather x1, waiting for transfers between devices, per_device(): lax.all_gather(down_blocks, 'dp', axis=0, tiled=True)  25.6 us
    all_gather x1, waiting for transfers between devices, per_device(): lax.all_gather(up_blocks, 'dp', axis=0, tiled=True)  25.2 us
    all_gather x1, waiting for transfers between devices, per_device(): lax.all_gather(gate_blocks, 'dp', axis=0, tiled=True)  22 us
    scatter-add x1, other arithmetic, per_device(): gate_pre = zero_cols.at[:, cols_here].add(gate_part)  18.7 us
    scatter-add x1, other arithmetic, per_device(): ffn3 = zero_rows.at[:, rows_here].add(product)  18.5 us
    scatter-add x1, other arithmetic, per_device(): grad_hidden = zero_cols.at[:, cols_here].add(product)  18.4 us
  transfers between devices with their start and end apart: 6, of which 5 were waited for; matrix products, arithmetic and copies ran while one was open for 25% of the time, Pallas kernels for 0%

commit v1 on v0

--- a/solution.py
+++ b/solution.py
@@ -50,7 +50,9 @@
     gate_all, up_all, down_all = (
         lax.all_gather(gate_blocks, "dp", axis=0, tiled=True),
         lax.all_gather(up_blocks, "dp", axis=0, tiled=True),
-        lax.all_gather(down_blocks, "dp", axis=0, tiled=True),
+        jnp.concatenate(
+            lax.all_to_all(jnp.stack([down_blocks] * lax.axis_size("dp")), "dp", 0, 0), axis=0
+        ),
     )
     pieces = (gate_all, up_all)
     rows_here, cols_here = select()

time: 659 us -> 630 us (0.956)
  waiting for transfers between devices: 339 us -> 299 us
  starting transfers between devices: 0.24 us -> 8.54 us
    all_gather x1 -> x0, waiting for transfers between devices: 25.6 us -> none  [per_device(): lax.all_gather(down_blocks, 'dp', axis=0, tiled=True)]
    all_gather x1, waiting for transfers between devices: 22 us -> 0.02 us  [per_device(): lax.all_gather(gate_blocks, 'dp', axis=0, tiled=True)]
    all_to_all x0 -> x1, waiting for transfers between devices: none -> 16.1 us  [per_device(): lax.all_to_all(jnp.stack([down_blocks] * lax.axis_size('dp')), 'dp', 0, 0)]
    all_to_all x0 -> x1, starting transfers between devices: none -> 8.34 us  [per_device(): lax.all_to_all(jnp.stack([down_blocks] * lax.axis_size('dp')), 'dp', 0, 0)]
    all_gather x1, waiting for transfers between devices: 25.2 us -> 17.5 us  [per_device(): lax.all_gather(up_blocks, 'dp', axis=0, tiled=True)]
    unnamed x7 -> x6, waiting for transfers between devices: 248 us -> 248 us
  transfers between devices with their start and end apart: 6 -> 6, of which waited for: 5 -> 4; matrix products, arithmetic and copies ran while one was open for 25% -> 27% of each run, Pallas kernels for 0% -> 0%
where the time goes in v1:
time: 630 us; the launch traced here: 621 us
  waiting for transfers between devices  299 us (47%)
  other arithmetic  137 us (22%)
  matrix products  83.9 us (13%)
  blocking collectives  37.2 us (6%)
  local copies, waits for them, and re-layouts  32 us (5%)
  between operations  22.7 us (4%)
  starting transfers between devices  8.54 us (1%)
    unnamed x6, waiting for transfers between devices  248 us
    psum x1, blocking collectives, per_device(): gain_sum, depth_sum = lax.psum((gain_part, jnp.stack(depth_list)), 'dp')  37.2 us
    scatter-add x1, other arithmetic, per_device(): grad_hidden = zero_cols.at[:, cols_here].add(product)  18.9 us
    scatter-add x1, other arithmetic, per_device(): ffn3 = zero_rows.at[:, rows_here].add(product)  18.5 us
    scatter-add x1, other arithmetic, per_device(): up_pre = zero_cols.at[:, cols_here].add(up_part)  18.4 us
    psum x1, waiting for transfers between devices, per_device(): lax.psum(grad_normed.astype(jnp.bfloat16), 'tensor').astype(jnp.float32)  18.3 us
    scatter-add x1, other arithmetic, per_device(): grad_normed3 = zero_rows.at[:, rows_here].add(contrib)  18.3 us
    scatter-add x1, other arithmetic, per_device(): gate_pre = zero_cols.at[:, cols_here].add(gate_part)  18.2 us
  transfers between devices with their start and end apart: 6, of which 4 were waited for; matrix products, arithmetic and copies ran while one was open for 27% of the time, Pallas kernels for 0%

profile of v1, /device:TPU:0, one launch (start us, length us, event | category | flops | bytes accessed | tf_op | source)
XLA Modules:
  0.0 620.9 jit_solution(16953657523187734614)
XLA Ops:
  7.2 0.0 all-gather.3.cloned.1.call-start
  7.2 0.7 all-gather.3.cloned.1.call-update
  7.9 0.0 all-gather.5.cloned.1.call-start
  7.9 0.7 all-gather.5.cloned.1.call-update
  8.7 3.6 stack.24
  12.3 8.3 %all-to-all-start = ((bf16[16,7,128,128]{3,2,1,0:T(8,128)(2,1)}), bf16[16,7,128,128]{3,2,1,0:T(8,128)(2,1)}, u32[]{:S(2)}, u32[]{:S(2)}) async-start(bf16[16,7,128,128]{3,2,1,0:T(8,128)(2,1)} %stack.24), calls=%async_computation | async-start | bytes 7340032 | tf_op jit(solution)/shard_map/all_to_all | solution.py:54
  20.6 0.0 all-reduce.5.cloned.1.call-start
  20.7 0.6 fusion.74
  29.1 0.6 fusion.75
  29.7 7.2 %fusion.43 = f32[24,8,32,128]{3,1,2,0:T(8,128)S(1)} fusion(f32[]{:T(128)} %bitcast.9, f32[]{:T(128)} %bitcast.6, f32[]{:T(128)} %bitcast.3, f32[]{:T(128)} %bitcast, bf16[4,192,4096]{2,1,0:T(8,128)(2,1)} %param.13, s32[]{:T(128)S(6)} %select_n.49, s32[]{:T(128)S(6)} %select_n.48, s32[]{:T(128)S(6)} %select_n.47, s32[]{:T(128)S(6)} %select_n.46), kind=kLoop, calls=%fused_computation.71 | loop fusion | flops 8650752 | bytes 9437216
  36.9 0.5 copy.31
  37.5 0.1 copy-done.10
  37.6 5.6 multiply_reduce_fusion
  43.3 2.0 fusion.49
  45.3 3.7 gather_fusion
  49.0 0.4 copy_bitcast_fusion.2
  49.4 3.7 gather_fusion.2
  53.2 16.1 %all-to-all-done = bf16[16,7,128,128]{3,2,1,0:T(8,128)(2,1)} async-done(((bf16[16,7,128,128]{3,2,1,0:T(8,128)(2,1)}), bf16[16,7,128,128]{3,2,1,0:T(8,128)(2,1)}, u32[]{:S(2)}, u32[]{:S(2)}) %all-to-all-start) | async-done | bytes 3670048 | tf_op jit(solution)/shard_map/all_to_all | solution.py:54
  69.2 10.4 %fusion.10 = f32[112,192,128]{2,1,0:T(8,128)} fusion(bf16[112,128,128]{2,1,0:T(8,128)(2,1)} %bitcast.19, bf16[112,192,128]{2,1,0:T(8,128)(2,1)} %gather_fusion.2, pred[112]{0:T(512)(128)(4,1)S(1)} %get-tuple-element.30), kind=kOutput, calls=%fused_computation.21 | convolution fusion | flops 707395584 | bytes 20185200 | tf_op jit(solution)/shard_map/tbj,bij->tbi/dot_general | solution.py:79
  79.6 0.1 broadcast_in_dim.37.clone.1
  79.7 18.9 %scatter_fusion.3 = f32[192,14,128]{2,0,1:T(8,128)S(1)} fusion(f32[192,14,128]{2,0,1:T(8,128)S(1)} %broadcast_in_dim.37.clone.1, s32[112]{0:T(128)S(1)} %get-tuple-element.32, f32[112,192,128]{2,1,0:T(8,128)} %fusion.10), kind=kCustom, calls=%fused_computation.8 | custom fusion | flops 2752512 | bytes 33030592 | tf_op jit(solution)/shard_map/scatter-add | solution.py:80
  98.6 0.0 all-gather.3.cloned.1.call-done
  98.7 9.7 %fusion.19 = f32[112,192,128]{2,1,0:T(8,128)} fusion(bf16[112,128,128]{2,1,0:T(8,128)(2,1)} %all-gather.3.cloned.1.call-done, bf16[112,192,128]{2,1,0:T(8,128)(2,1)} %gather_fusion, pred[112]{0:T(512)(128)(4,1)S(1)} %get-tuple-element.30), kind=kOutput, calls=%fused_computation.30 | convolution fusion | flops 707395584 | bytes 20185200 | tf_op jit(solution)/shard_map/tbi,bij->tbj/dot_general | solution.py:60
  108.3 0.1 broadcast_in_dim.37.clone
  108.5 18.2 %scatter_fusion = f32[192,14,128]{2,0,1:T(8,128)S(1)} fusion(f32[192,14,128]{2,0,1:T(8,128)S(1)} %broadcast_in_dim.37.clone, s32[112]{0:T(128)S(1)} %get-tuple-element.32, f32[112,192,128]{2,1,0:T(8,128)} %fusion.19), kind=kCustom, calls=%fused_computation.5 | custom fusion | flops 2752512 | bytes 33030592 | tf_op jit(solution)/shard_map/scatter-add | solution.py:62
  126.7 17.5 %all-gather.5.cloned.1.call-done = bf16[112,128,128]{2,1,0:T(8,128)(2,1)} async-done(((bf16[7,128,128]{2,1,0:T(8,128)(2,1)}), bf16[112,128,128]{2,1,0:T(8,128)(2,1)}) %all-gather.5.cloned.1.call-update) | async-done | bytes 3670032 | tf_op jit(solution)/shard_map/all_gather | solution.py:52
  144.2 9.5 %fusion.17 = f32[112,192,128]{2,1,0:T(8,128)} fusion(bf16[112,128,128]{2,1,0:T(8,128)(2,1)} %all-gather.5.cloned.1.call-done, bf16[112,192,128]{2,1,0:T(8,128)(2,1)} %gather_fusion, pred[112]{0:T(512)(128)(4,1)S(1)} %get-tuple-element.30), kind=kOutput, calls=%fused_computation.28 | convolution fusion | flops 707395584 | bytes 20185200 | tf_op jit(solution)/shard_map/tbi,bij->tbj/dot_general | solution.py:61
  153.7 0.1 broadcast_in_dim.37.clone.2
  153.8 18.4 %scatter_fusion.1 = f32[192,14,128]{2,0,1:T(8,128)S(1)} fusion(f32[192,14,128]{2,0,1:T(8,128)S(1)} %broadcast_in_dim.37.clone.2, s32[112]{0:T(128)S(1)} %get-tuple-element.32, f32[112,192,128]{2,1,0:T(8,128)} %fusion.17), kind=kCustom, calls=%fused_computation.6 | custom fusion | flops 2752512 | bytes 33030592 | tf_op jit(solution)/shard_map/scatter-add | solution.py:63
  172.2 3.4 multiply_convert_fusion.1
  175.5 4.8 gather_fusion.4
  180.3 3.8 gather_fusion.3
  184.1 10.5 %fusion.2 = f32[112,192,128]{2,1,0:T(8,128)} fusion(bf16[112,128,128]{2,1,0:T(8,128)(2,1)} %all-gather.5.cloned.1.call-done, bf16[112,192,128]{2,1,0:T(8,128)(2,1)} %gather_fusion.4, pred[112]{0:T(512)(128)(4,1)S(1)} %get-tuple-element.18), kind=kOutput, calls=%fused_computation.13 | convolution fusion | flops 707395584 | bytes 20185200 | tf_op jit(solution)/shard_map/tbj,bij->tbi/dot_general | solution.py:91
  194.6 12.1 %fusion.29 = f32[112,192,128]{2,1,0:T(8,128)} fusion(f32[112,192,128]{2,1,0:T(8,128)} %fusion.2, bf16[112,128,128]{2,1,0:T(8,128)(2,1)} %all-gather.3.cloned.1.call-done, bf16[112,192,128]{2,1,0:T(8,128)(2,1)S(1)} %copy-done.3, pred[112]{0:T(512)(128)(4,1)S(1)} %get-tuple-element.18), kind=kOutput, calls=%fused_computation.56 | convolution fusion | flops 710148096 | bytes 31195248 | tf_op jit(solution)/shard_map/tbj,bij->tbi/dot_general | solution.py:90
  206.6 0.3 broadcast_in_dim.36.clone.1
  207.0 18.3 %scatter_fusion.4 = f32[192,32,128]{2,0,1:T(8,128)S(1)} fusion(f32[192,32,128]{2,0,1:T(8,128)S(1)} %broadcast_in_dim.36.clone.1, s32[112]{0:T(128)S(1)} %get-tuple-element.33, f32[112,192,128]{2,1,0:T(8,128)} %fusion.29), kind=kCustom, calls=%fused_computation.9 | custom fusion | flops 2752512 | bytes 33030592 | tf_op jit(solution)/shard_map/scatter-add | solution.py:94
  225.2 1.3 copy_bitcast_fusion
  226.6 0.0 all-reduce.5.cloned.1.call-update
  226.6 0.0 reduce-scatter.5.cloned.1.call-start
  226.7 1.0 copy-done.1
  227.7 3.8 gather_fusion.1
  231.5 9.7 %fusion.13 = f32[112,192,128]{2,1,0:T(8,128)} fusion(bf16[112,128,128]{2,1,0:T(8,128)(2,1)} %bitcast.19, bf16[112,192,128]{2,1,0:T(8,128)(2,1)} %gather_fusion.1, pred[112]{0:T(512)(128)(4,1)S(1)} %get-tuple-element.18), kind=kOutput, calls=%fused_computation.24 | convolution fusion | flops 707395584 | bytes 20185200 | tf_op jit(solution)/shard_map/tbi,bij->tbj/dot_general | solution.py:67
  241.2 0.3 broadcast_in_dim.36.clone
  241.5 18.5 %scatter_fusion.2 = f32[192,32,128]{2,0,1:T(8,128)S(1)} fusion(f32[192,32,128]{2,0,1:T(8,128)S(1)} %broadcast_in_dim.36.clone, s32[112]{0:T(128)S(1)} %get-tuple-element.33, f32[112,192,128]{2,1,0:T(8,128)} %fusion.13), kind=kCustom, calls=%fused_computation.7 | custom fusion | flops 2752512 | bytes 33030592 | tf_op jit(solution)/shard_map/scatter-add | solution.py:68
  260.1 1.4 copy_bitcast_fusion.1
  261.5 0.0 reduce-scatter.5.cloned.1.call-update
  261.5 0.0 all-reduce.7.cloned.1.call-start
  261.6 8.8 %convert_bitcast_fusion.5 = bf16[112,1,128,128]{3,2,0,1:T(8,128)(2,1)} fusion(bf16[112,192,128]{2,1,0:T(8,128)(2,1)} %gather_fusion.4, pred[112]{0:T(512)(128)(4,1)S(1)} %get-tuple-element.18, bf16[112,192,128]{2,1,0:T(8,128)(2,1)} %gather_fusion, pred[112]{0:T(512)(128)(4,1)S(1)} %get-tuple-element.30), kind=kOutput, calls=%fused_computation.60 | convolution fusion | flops 711983104 | bytes 14680288 | tf_op jit(solution)/shard_map/tbi,tbj->bij/dot_general | solution.py:104
  270.3 8.8 %convert_bitcast_fusion.6 = bf16[112,1,128,128]{3,2,0,1:T(8,128)(2,1)} fusion(bf16[112,192,128]{2,1,0:T(8,128)(2,1)} %gather_fusion.3, pred[112]{0:T(512)(128)(4,1)S(1)} %get-tuple-element.18, bf16[112,192,128]{2,1,0:T(8,128)(2,1)} %gather_fusion, pred[112]{0:T(512)(128)(4,1)S(1)} %get-tuple-element.30), kind=kOutput, calls=%fused_computation.61 | convolution fusion | flops 711983104 | bytes 14680288 | tf_op jit(solution)/shard_map/tbi,tbj->bij/dot_general | solution.py:101
  279.2 4.5 convert_bitcast_fusion.4
  283.7 9.7 %pad_maximum_fusion = bf16[112,3,128,128]{3,2,0,1:T(8,128)(2,1)} fusion(bf16[112,1,128,128]{3,2,0,1:T(8,128)(2,1)} %convert_bitcast_fusion.4, bf16[112,1,128,128]{3,2,0,1:T(8,128)(2,1)} %convert_bitcast_fusion.5, bf16[112,1,128,128]{3,2,0,1:T(8,128)(2,1)} %convert_bitcast_fusion.6), kind=kLoop, calls=%fused_computation.10 | loop fusion | flops 11010048 | bytes 22020096 | tf_op jit(solution)/shard_map/stack | solution.py:109
  293.5 0.6 copy-done.11
  294.1 0.6 dynamic-slice.2
  294.7 18.3 %all-reduce.5.cloned.1.call-done = bf16[192,4096]{1,0:T(8,128)(2,1)} async-done(((bf16[192,4096]{1,0:T(8,128)(2,1)}), bf16[192,4096]{1,0:T(8,128)(2,1)}) %all-reduce.5.cloned.1.call-update) | async-done | bytes 1572880 | tf_op jit(solution)/shard_map/psum | solution.py:115
  313.0 2.8 fusion.35
  315.8 0.1 dynamic_slice.32
  315.9 5.9 fusion.39
  321.8 2.7 pad_maximum_fusion.1
  325.1 37.2 %all-reduce.1 = (f32[4]{0:T(128)}, f32[512]{0:T(512)}) all-reduce(f32[4]{0:T(128)S(1)} %pad_maximum_fusion.1, f32[512]{0:T(512)S(1)} %dynamic_slice.32), channel_id=1, replica_groups=mesh['dp'=16,'tensor'=8] {'dp'}, use_global_device_ids=true, to_apply=%region_14.17 | all-reduce | flops 516 | bytes 4128 | tf_op jit(solution)/shard_map/psum | solution.py:125
  362.3 1.8 constant_dynamic-slice_fusion
  364.1 1.6 add_convert_fusion
  365.7 246.1 %all-reduce.7.cloned.1.call-done = bf16[112,3,128,128]{3,2,0,1:T(8,128)(2,1)} async-done(((bf16[112,3,128,128]{3,2,0,1:T(8,128)(2,1)}), bf16[112,3,128,128]{3,2,0,1:T(8,128)(2,1)}) %all-reduce.7.cloned.1.call-update) | async-done | bytes 11010064
  611.8 1.2 dynamic-slice_convert_fusion
  613.1 1.1 slice_bitcast_fusion
  (43 shorter events, 0.1 us)
Async XLA Ops:
  7.2 91.5 %all-gather.3.cloned.1.call-start = ((), (), s32[]{:S(2)}) async-start(), calls=%async_computation.2 | async-start | bytes 3899392 | tf_op jit(solution)/shard_map/all_gather | solution.py:51
  7.9 136.2 %all-gather.5.cloned.1.call-start = ((), (), s32[]{:S(2)}) async-start(), calls=%async_computation.3 | async-start | bytes 3899392 | tf_op jit(solution)/shard_map/all_gather | solution.py:52
  12.3 8.4 %copy-start.8 = (s32[4]{0:T(128)S(1)}, s32[4]{0:T(128)}, u32[]{:S(2)}) copy-start(s32[4]{0:T(128)} %param.15) | copy-start | bytes 52
  12.3 16.8 %copy-start.9 = (f32[4]{0:T(128)S(1)}, f32[4]{0:T(128)}, u32[]{:S(2)}) copy-start(f32[4]{0:T(128)} %param.14) | copy-start | bytes 52
  12.3 56.9 %all-to-all-start = ((bf16[16,7,128,128]{3,2,1,0:T(8,128)(2,1)}), bf16[16,7,128,128]{3,2,1,0:T(8,128)(2,1)}, u32[]{:S(2)}, u32[]{:S(2)}) async-start(bf16[16,7,128,128]{3,2,1,0:T(8,128)(2,1)} %stack.24), calls=%async_computation | async-start | bytes 7340032 | tf_op jit(solution)/shard_map/all_to_all | solution.py:54
  20.6 292.3 %all-reduce.5.cloned.1.call-start = ((), (), s32[]{:S(2)}) async-start(), calls=%async_computation.5 | async-start | bytes 3145728 | tf_op jit(solution)/shard_map/psum | solution.py:115
  29.7 7.9 %slice-start = ((s8[6291456]{0:T(1024)(128)(4,1)}), s8[4194304]{0:T(1024)(128)(4,1)S(1)}, s32[]{:S(2)}) async-start(s8[6291456]{0:T(1024)(128)(4,1)} %bitcast.159), calls=%async_computation.7 | async-start | bytes 8388608
  29.7 7.9 %slice-start.1 = ((s8[6291456]{0:T(1024)(128)(4,1)}), s8[2097152]{0:T(1024)(128)(4,1)S(1)}, s32[]{:S(2)}) async-start(s8[6291456]{0:T(1024)(128)(4,1)} %bitcast.159), calls=%async_computation.8 | async-start | bytes 4194304
  36.9 0.7 copy-start.10
  37.6 5.6 copy-start.7
  45.3 3.7 copy-start.4
  126.7 17.5 %copy-start = (f32[192,14,128]{2,0,1:T(8,128)}, f32[192,14,128]{2,0,1:T(8,128)S(1)}, u32[]{:S(2)}) copy-start(f32[192,14,128]{2,0,1:T(8,128)S(1)} %scatter_fusion) | copy-start | bytes 4128772
  184.1 10.5 %copy-start.3 = (bf16[112,192,128]{2,1,0:T(8,128)(2,1)S(1)}, bf16[112,192,128]{2,1,0:T(8,128)(2,1)}, u32[]{:S(2)}) copy-start(bf16[112,192,128]{2,1,0:T(8,128)(2,1)} %gather_fusion.3) | copy-start | bytes 16515076
  226.6 1.1 copy-start.1
  226.6 137.5 %reduce-scatter.5.cloned.1.call-start = ((), (), s32[]{:S(2)}) async-start(), calls=%async_computation.4 | async-start | bytes 1769472 | tf_op jit(solution)/shard_map/reduce_scatter | solution.py:69
  261.5 350.3 %all-reduce.7.cloned.1.call-start = ((), (), s32[]{:S(2)}) async-start(), calls=%async_computation.6 | async-start | bytes 22020096
  261.5 17.6 %slice-start.2 = ((s8[5505024]{0:T(1024)(128)(4,1)}), s8[4194304]{0:T(1024)(128)(4,1)S(1)}, s32[]{:S(2)}) async-start(s8[5505024]{0:T(1024)(128)(4,1)} %bitcast.161), calls=%async_computation.9 | async-start | bytes 8388608
  261.5 17.6 %slice-start.4 = ((s8[5505024]{0:T(1024)(128)(4,1)}), s8[4194304]{0:T(1024)(128)(4,1)S(1)}, s32[]{:S(2)}) async-start(s8[5505024]{0:T(1024)(128)(4,1)} %bitcast.163), calls=%async_computation.11 | async-start | bytes 8388608
  270.3 8.8 %slice-start.3 = ((s8[5505024]{0:T(1024)(128)(4,1)}), s8[1310720]{0:T(1024)(128)(4,1)S(1)}, s32[]{:S(2)}) async-start(s8[5505024]{0:T(1024)(128)(4,1)} %bitcast.161), calls=%async_computation.10 | async-start | bytes 2621440
  270.3 8.8 %slice-start.5 = ((s8[5505024]{0:T(1024)(128)(4,1)}), s8[1310720]{0:T(1024)(128)(4,1)S(1)}, s32[]{:S(2)}) async-start(s8[5505024]{0:T(1024)(128)(4,1)} %bitcast.163), calls=%async_computation.12 | async-start | bytes 2621440
  293.4 0.7 copy-start.11
  293.4 19.6 %copy-start.2 = (f32[192,4096]{1,0:T(8,128)S(1)}, f32[192,4096]{1,0:T(8,128)}, u32[]{:S(2)}) copy-start(f32[192,4096]{1,0:T(8,128)} %get-tuple-element.23) | copy-start | bytes 9437188
  313.0 2.9 copy-start.5
  313.0 2.9 copy-start.6
Sparse Core Ops, SparseCore 0:
  10.4 80.1 all-gather.2
  93.1 50.9 all-gather.4
  226.7 86.1 all-reduce.4
  315.2 45.4 reduce-scatter.4
  363.1 248.6 all-reduce.6
